TPU v7x, 32 devices: a whole 2x2x4 slice. The times are simulated.
32 devices in a mesh: row: 4 (over y, x), col: 8 (over z, core).
Axes of the slice: x: 2, y: 2, z: 4, core: 2. Of those that a mesh axis runs over, the one named last changes fastest.
Arguments:
- anc_inverse: float32 [10240, 10240], P('row', 'col'), may hold values from -0.0625 to 0.0625
- lower_anc: float32 [10240, 3, 384], P('col', None, 'row'), may hold values from -1.5 to 1.5
- upper_anc: float32 [10240, 3, 384], P('row', None, 'col'), may hold values from -0.75 to 0.75
- lower_edge: float32 [2, 384, 384], replicated, may hold values from -0.3125 to 0.3125
- upper_edge: float32 [2, 384, 384], replicated, may hold values from -0.3125 to 0.3125
- diag_inverse: float32 [3, 384, 384], replicated, may hold values from -6 to 6
- tile_mask: int32 [3, 80, 3], replicated, may hold values 0 or 1
Outputs:
- x_blocks: float32 [10240, 3, 384], P(('row', 'col'))
- y_blocks: float32 [8, 4, 320, 3, 384], P('col', 'row')
- z_blocks: float32 [3, 384, 384], P(None, 'row', 'col')
- cross_blocks: float32 [2, 2, 384, 384], P(None, None, 'row', 'col')
All inputs are finite; a program needn't handle non-finite values.
Results may differ from a plain program's by a relative error of at most 0.0001.
Values sent between devices are 32-bit elements; how exact they have to be, the bound alone decides.
A program may use at most 128 MiB of HBM per device.

v0:
```python
import jax
import jax.numpy as jnp
from jax import lax
from jax.sharding import PartitionSpec as P

W = 384
BLK = 128
SUPER = 3
precise = lax.Precision.HIGHEST


def product(left, right):
    return jnp.dot(left, right, precision=precise, preferred_element_type=jnp.float32)


def inner_product(left, right):
    return lax.dot_general(
        left, right, (((0,), (0,)), ((), ())), precision=precise, preferred_element_type=jnp.float32
    )


def outer_product(left, right):
    return lax.dot_general(
        left, right, (((1,), (1,)), ((), ())), precision=precise, preferred_element_type=jnp.float32
    )


def tile_pattern(tile_mask, first_block, blocks):
    window = lax.dynamic_slice_in_dim(tile_mask, first_block, blocks, 1).astype(jnp.float32)
    window = jnp.transpose(window, (1, 0, 2))
    widened = jnp.broadcast_to(window[:, None, :, :, None], (blocks, BLK, SUPER, W // BLK, BLK))
    return widened.reshape(blocks * BLK, SUPER, W)


def row_term(anc_inverse, lower_cols):
    return product(anc_inverse, lower_cols)


def col_term(anc_inverse, upper_rows):
    return inner_product(anc_inverse, upper_rows)


def per_device(anc_inverse, lower_anc, upper_anc, lower_edge, upper_edge, diag_inverse, tile_mask):
    rows_here, cols_here = anc_inverse.shape
    slab_rows = rows_here // lax.axis_size("col")
    row_index = lax.axis_index("row")
    col_index = lax.axis_index("col")
    col_pattern = tile_pattern(tile_mask, col_index * (cols_here // BLK), cols_here // BLK)
    row_pattern = tile_pattern(tile_mask, row_index * (rows_here // BLK), rows_here // BLK)
    lower_list = []
    upper_list = []
    cols_list = []
    rows_list = []
    lower_full = lax.all_gather(lower_anc, "row", axis=2, tiled=True) * col_pattern
    upper_full = lax.all_gather(upper_anc, "col", axis=2, tiled=True) * row_pattern
    cols_all = lax.psum_scatter(
        row_term(anc_inverse, lower_full.reshape(cols_here, SUPER * W)),
        "col",
        scatter_dimension=0,
        tiled=True,
    )
    rows_all = lax.psum_scatter(
        col_term(anc_inverse, upper_full.reshape(rows_here, SUPER * W)),
        "row",
        scatter_dimension=0,
        tiled=True,
    )
    cols_all = cols_all.reshape(slab_rows, SUPER, W)
    rows_all = rows_all.reshape(slab_rows, SUPER, W)
    for node_index in range(SUPER):
        lower_list.append(lower_full[:, node_index, :])
        upper_list.append(upper_full[:, node_index, :])
        cols_list.append(cols_all[:, node_index, :])
        rows_list.append(rows_all[:, node_index, :])
    x_list = []
    y_list = []
    corner_list = []
    cross_cols = []
    cross_rows = []
    for node_index in range(SUPER):
        lower_cur = lower_list[node_index]
        upper_cur = upper_list[node_index]
        inv_cols = -cols_list[node_index]
        inv_rows = -rows_list[node_index]
        upper_mine = lax.dynamic_slice_in_dim(upper_cur, col_index * slab_rows, slab_rows, 0)
        if node_index > 0:
            lower_side = lower_edge[node_index - 1]
            upper_side = upper_edge[node_index - 1]
            lower_mine = lax.dynamic_slice_in_dim(lower_cur, row_index * slab_rows, slab_rows, 0)
            rows_lower = inner_product(prev_rows, lower_mine)
            upper_cols = inner_product(upper_mine, prev_cols)
        if node_index > 0:
            rows_lower, upper_cols = lax.psum((rows_lower, upper_cols), ("row", "col"))
        if node_index > 0:
            cross_col = -(rows_lower + product(prev_corner, lower_side))
            cross_row = -(upper_cols + product(upper_side, prev_corner))
            inv_cols = inv_cols - product(prev_cols, lower_side)
            inv_rows = inv_rows - outer_product(prev_rows, upper_side)
            cross_cols.append(cross_col)
            cross_rows.append(cross_row)
        inv_corner = diag_inverse[node_index] - lax.psum(
            inner_product(upper_mine, inv_cols), ("row", "col")
        )
        if node_index > 0:
            inv_corner = inv_corner - product(upper_side, cross_col)
        x_list.append(inv_cols)
        y_list.append(inv_rows)
        corner_list.append(inv_corner)
        prev_cols = inv_cols
        prev_rows = inv_rows
        prev_corner = inv_corner
    x_blocks = jnp.stack(x_list, axis=1)
    y_blocks = jnp.stack(y_list, axis=1)[None, None]
    tile_rows = W // lax.axis_size("row")
    tile_cols = W // lax.axis_size("col")
    corners = jnp.stack(corner_list)
    corners = lax.dynamic_slice_in_dim(corners, row_index * tile_rows, tile_rows, 1)
    z_blocks = lax.dynamic_slice_in_dim(corners, col_index * tile_cols, tile_cols, 2)
    crossed = jnp.stack([jnp.stack(cross_cols), jnp.stack(cross_rows)])
    crossed = lax.dynamic_slice_in_dim(crossed, row_index * tile_rows, tile_rows, 2)
    cross_blocks = lax.dynamic_slice_in_dim(crossed, col_index * tile_cols, tile_cols, 3)
    return (x_blocks, y_blocks, z_blocks, cross_blocks)


def solution(mesh):
    return jax.shard_map(
        per_device,
        mesh=mesh,
        in_specs=(
            P("row", "col"),
            P("col", None, "row"),
            P("row", None, "col"),
            P(),
            P(),
            P(),
            P(),
        ),
        out_specs=(
            P(("row", "col"), None, None),
            P("col", "row", None, None, None),
            P(None, "row", "col"),
            P(None, None, "row", "col"),
        ),
        check_vma=False,
    )
```

profile of v0, /device:TPU:0, one launch (start us, length us, event | category | flops | bytes accessed | tf_op | source)
XLA Modules:
  0.0 565.6 jit_solution(17613502817447202190)
XLA Ops:
  8.9 4.2 broadcast_in_dim.6
  13.1 10.5 %reshape.42 = f32[1280,3,384]{2,0,1:T(8,128)} reshape(f32[10,128,3,3,128]{4,3,1,0,2:T(4,128)} %broadcast_in_dim.6) | data formatting | bytes 11796480 | tf_op jit(solution)/shard_map/reshape | solution.py:32
  23.6 55.8 %all-gather.3.cloned.1.call-done = f32[1280,3,384]{0,2,1:T(8,128)} async-done(((f32[1280,3,96]{0,2,1:T(8,128)}), f32[1280,3,384]{0,2,1:T(8,128)}) %all-gather.3.cloned.1.call-update) | async-done | bytes 5898256 | tf_op jit(solution)/shard_map/all_gather | solution.py:54
  79.3 7.7 %copy.70 = f32[1280,3,384]{2,0,1:T(8,128)} copy(f32[1280,3,384]{0,2,1:T(8,128)} %all-gather.3.cloned.1.call-done) | data formatting | bytes 11796480 | tf_op jit(solution)/shard_map/all_gather | solution.py:54
  87.0 9.3 %mul.30 = f32[1280,3,384]{2,0,1:T(8,128)} multiply(f32[1280,3,384]{2,0,1:T(8,128)} %copy.70, f32[1280,3,384]{2,0,1:T(8,128)} %reshape.42) | non-fusion elementwise | flops 1474560 | bytes 17694720 | tf_op jit(solution)/shard_map/mul | solution.py:54
  96.3 7.8 %copy.71 = f32[1280,3,384]{0,2,1:T(8,128)} copy(f32[1280,3,384]{2,0,1:T(8,128)} %mul.30) | data formatting | bytes 11796480 | tf_op jit(solution)/shard_map/mul | solution.py:54
  104.0 52.7 %convolution_bitcast_fusion = f32[2560,1152]{0,1:T(8,128)} fusion(f32[1280,1152]{0,1:T(8,128)} %bitcast.163, f32[2560,1280]{1,0:T(8,128)} %param.7), kind=kOutput, calls=%fused_computation | convolution fusion | flops 45298483200 | bytes 30801920 | tf_op jit(solution)/shard_map/dot_general | solution.py:13
  156.8 13.6 %copy.92 = f32[2560,1152]{1,0:T(8,128)} copy(f32[2560,1152]{0,1:T(8,128)} %convolution_bitcast_fusion) | data formatting | bytes 23592960
  171.1 6.0 %broadcast_in_dim.7 = f32[20,128,3,3,128]{1,0,4,3,2:T(8,128)} broadcast(f32[20,3,3]{0,2,1:T(4,128)S(1)} %convert_bitcast_fusion), dimensions={0,2,3} | broadcast | bytes 11797200 | tf_op jit(solution)/shard_map/broadcast_in_dim | solution.py:31
  177.1 13.7 %reshape.45 = f32[2560,3,384]{0,2,1:T(8,128)} reshape(f32[20,128,3,3,128]{1,0,4,3,2:T(8,128)} %broadcast_in_dim.7) | data formatting | bytes 23592960 | tf_op jit(solution)/shard_map/reshape | solution.py:32
  191.2 9.7 %mul.32 = f32[2560,3,384]{0,2,1:T(8,128)S(1)} multiply(f32[2560,3,384]{0,2,1:T(8,128)} %all-gather.5.cloned.1.call-done, f32[2560,3,384]{0,2,1:T(8,128)} %reshape.45) | non-fusion elementwise | flops 2949120 | bytes 35389440 | tf_op jit(solution)/shard_map/mul | solution.py:55
  200.9 4.3 copy-done
  205.3 50.1 %convolution_bitcast_fusion.1 = f32[1280,1152]{0,1:T(8,128)} fusion(f32[2560,1152]{0,1:T(8,128)S(1)} %bitcast.157, f32[2560,1280]{1,0:T(8,128)} %param.7), kind=kOutput, calls=%fused_computation.1 | convolution fusion | flops 45298483200 | bytes 30801920 | tf_op jit(solution)/shard_map/dot_general | solution.py:17
  255.4 7.7 %copy.94 = f32[1280,1152]{1,0:T(8,128)} copy(f32[1280,1152]{0,1:T(8,128)} %convolution_bitcast_fusion.1) | data formatting | bytes 11796480
  263.3 4.3 fusion.75
  267.6 9.3 %fusion.74 = (f32[2560,1,384]{0,2,1:T(8,128)}, f32[2560,1,384]{0,2,1:T(8,128)}, f32[2560,1,384]{0,2,1:T(8,128)}) fusion(f32[2560,3,384]{0,2,1:T(8,128)} %copy-done), kind=kLoop, calls=%fused_computation.100 | loop fusion | bytes 23592960 | tf_op jit(solution)/shard_map/slice | solution.py:72
  276.9 36.6 %reduce-scatter.7.cloned.1.call-done = f32[320,1152]{1,0:T(8,128)} async-done(((f32[2560,1152]{1,0:T(8,128)}), f32[320,1152]{1,0:T(8,128)}) %reduce-scatter.7.cloned.1.call-update) | async-done | bytes 1474576
  313.5 2.1 copy.93
  315.6 0.9 fusion.77
  316.6 1.3 copy.96
  317.8 1.0 copy.97
  319.1 3.3 fusion.16
  322.4 1.1 convolution_subtract_fusion.3
  323.5 3.3 fusion.18
  326.7 3.3 fusion.12
  330.0 1.1 convolution_subtract_fusion.2
  331.9 3.2 fusion.14
  335.1 46.5 %reduce-scatter.9.cloned.1.call-done = f32[320,1152]{1,0:T(8,128)} async-done(((f32[1280,1152]{1,0:T(8,128)}), f32[320,1152]{1,0:T(8,128)}) %reduce-scatter.9.cloned.1.call-update) | async-done | bytes 1474576
  381.6 2.3 copy.95
  384.0 1.3 fusion.76
  385.2 1.4 copy.99
  386.6 2.1 copy.100
  388.7 3.3 fusion.20
  392.0 1.1 convolution_subtract_fusion.1
  393.1 3.2 fusion.49
  396.3 3.2 fusion.47
  401.2 1.3 copy.101
  402.5 2.2 pad_maximum_fusion
  404.7 1.1 fusion.11
  405.8 1.2 maximum_bitcast_fusion
  407.0 137.7 %all-reduce.3.cloned.1.call-done = (f32[384,384]{1,0:T(8,128)}, f32[384,384]{1,0:T(8,128)}, f32[384,384]{1,0:T(8,128)}, f32[384,384]{1,0:T(8,128)}, f32[384,384]...) async-done(((f32[384,384]{1,0:T(8,128)}, f32[384,384]{1,0:T(8,128)}, f32[384,384]{1,0:T(8,128)}, f32[384,384]{1,0:T(8,128)}, f32[384,384]{1,0:T(8,128)}, ...) | async-done | bytes 4128784 | tf_op jit(solution)/shard_map/psum | solution.py:101
  544.7 1.4 fusion.73
  546.3 2.5 fusion.7
  548.9 1.3 fusion
  550.2 1.3 fusion.10
  551.5 1.6 fusion.4
  553.1 1.3 fusion.1
  555.4 2.5 fusion.9
  (55 shorter events, 7.7 us)
Async XLA Ops:
  7.2 1.5 copy-start.16
  7.2 72.2 %all-gather.3.cloned.1.call-start = ((), (), s32[]{:S(2)}) async-start(), calls=%async_computation.2 | async-start | bytes 7372800 | tf_op jit(solution)/shard_map/all_gather | solution.py:54
  7.9 183.3 %all-gather.5.cloned.1.call-start = ((), (), s32[]{:S(2)}) async-start(), calls=%async_computation.3 | async-start | bytes 13271040 | tf_op jit(solution)/shard_map/all_gather | solution.py:55
  8.7 304.8 %reduce-scatter.7.cloned.1.call-start = ((), (), s32[]{:S(2)}) async-start(), calls=%async_computation.4 | async-start | bytes 13271040
  170.4 211.2 %reduce-scatter.9.cloned.1.call-start = ((), (), s32[]{:S(2)}) async-start(), calls=%async_computation.5 | async-start | bytes 7372800
  200.9 4.3 copy-start
  263.1 281.6 %all-reduce.3.cloned.1.call-start = ((), (), s32[]{:S(2)}) async-start(), calls=%async_computation.6 | async-start | bytes 8257536 | tf_op jit(solution)/shard_map/psum | solution.py:101
  317.8 4.5 copy-start.4
  319.1 3.3 copy-start.9
  331.1 0.8 copy-start.6
  385.2 6.8 %copy-start.1 = (f32[2,384,384]{2,1,0:T(8,128)S(1)}, f32[2,384,384]{2,1,0:T(8,128)}, u32[]{:S(2)}) copy-start(f32[2,384,384]{2,1,0:T(8,128)} %param.11) | copy-start | bytes 3538948
  388.7 3.3 copy-start.10
  400.4 2.1 copy-start.7
  404.7 1.1 copy-start.8
  544.7 1.5 copy-start.2
  544.7 1.6 copy-start.15
  544.7 4.2 copy-start.14
  546.1 2.7 copy-start.3
  546.1 2.7 copy-start.5
  548.8 1.3 copy-start.13
  550.1 1.3 copy-start.12
  551.5 1.6 copy-start.11
Sparse Core Ops, SparseCore 0:
  9.8 69.4 all-gather.2
  81.0 110.1 all-gather.4
  193.5 119.9 reduce-scatter.6
  316.4 65.2 reduce-scatter.8
  399.6 144.9 all-reduce.2
where the time goes:
time: 574 us; the launch traced here: 566 us
  waiting for transfers between devices  278 us (48%)
  matrix products  140 us (24%)
  local copies, waits for them, and re-layouts  105 us (18%)
  other arithmetic  26.1 us (5%)
  between operations  14.4 us (3%)
    psum x1, waiting for transfers between devices, per_device(): lax.psum(inner_product(upper_mine, inv_cols), ('row', 'col'))  138 us
    unnamed x7, waiting for transfers between devices  84.6 us
    dot_general x8, matrix products, inner_product(): lax.dot_general(left, right, (((0,), (0,)), ((), ())), precision=precise,...  72.9 us
    dot_general x9, matrix products, product(): jnp.dot(left, right, precision=precise, preferred_element_type=jnp.float32)  65.3 us
    all_gather x1, waiting for transfers between devices, per_device(): lax.all_gather(lower_anc, 'row', axis=2, tiled=True) * col_pattern  55.8 us
    unnamed x46, local copies, waits for them, and re-layouts  39.8 us
    reshape x2, local copies, waits for them, and re-layouts, tile_pattern(): return widened.reshape(blocks * BLK, SUPER, W)  24.2 us
  transfers between devices with their start and end apart: 5, of which 5 were waited for; matrix products, arithmetic and copies ran while one was open for 42% of the time, Pallas kernels for 0%

commit v1 on v0

--- a/solution.py
+++ b/solution.py
@@ -7,6 +7,12 @@
 BLK = 128
 SUPER = 3
 precise = lax.Precision.HIGHEST
+
+
+def add_all(x, axis):
+    parts = lax.all_gather(x, axis, axis=0, tiled=False)
+    acc = parts.sum(axis=0)
+    return acc
 
 
 def product(left, right):
@@ -98,7 +104,7 @@
             inv_rows = inv_rows - outer_product(prev_rows, upper_side)
             cross_cols.append(cross_col)
             cross_rows.append(cross_row)
-        inv_corner = diag_inverse[node_index] - lax.psum(
+        inv_corner = diag_inverse[node_index] - add_all(
             inner_product(upper_mine, inv_cols), ("row", "col")
         )
         if node_index > 0:

time: 574 us -> 930 us (1.62)
  waiting for transfers between devices: 278 us -> 596 us
  other arithmetic: 26.1 us -> 49.4 us
  local copies, waits for them, and re-layouts: 105 us -> 117 us
    all_gather x0 -> x3, waiting for transfers between devices: none -> 313 us  [add_all(): parts = lax.all_gather(x, axis, axis=0, tiled=False)]
    reduce_sum x0 -> x3, other arithmetic: none -> 22.6 us  [add_all(): acc = parts.sum(axis=0)]
    unnamed x7 -> x10, waiting for transfers between devices: 84.6 us -> 94.6 us
    unnamed x46 -> x44, local copies, waits for them, and re-layouts: 39.8 us -> 44.9 us
  transfers between devices with their start and end apart: 5 -> 8, of which waited for: 5 -> 8; matrix products, arithmetic and copies ran while one was open for 42% -> 32% of each run, Pallas kernels for 0% -> 0%
where the time goes in v1:
time: 930 us; the launch traced here: 922 us
  waiting for transfers between devices  596 us (64%)
  matrix products  143 us (15%)
  local copies, waits for them, and re-layouts  117 us (13%)
  other arithmetic  49.4 us (5%)
  between operations  14.7 us (2%)
    all_gather x3, waiting for transfers between devices, add_all(): parts = lax.all_gather(x, axis, axis=0, tiled=False)  313 us
    psum x1, waiting for transfers between devices, per_device(): rows_lower, upper_cols = lax.psum((rows_lower, upper_cols), ('row', 'col'))  131 us
    unnamed x10, waiting for transfers between devices  94.6 us
    dot_general x8, matrix products, inner_product(): lax.dot_general(left, right, (((0,), (0,)), ((), ())), precision=precise,...  73 us
    dot_general x9, matrix products, product(): jnp.dot(left, right, precision=precise, preferred_element_type=jnp.float32)  68.1 us
    all_gather x1, waiting for transfers between devices, per_device(): lax.all_gather(lower_anc, 'row', axis=2, tiled=True) * col_pattern  55.8 us
    unnamed x44, local copies, waits for them, and re-layouts  44.9 us
    reshape x2, local copies, waits for them, and re-layouts, tile_pattern(): return widened.reshape(blocks * BLK, SUPER, W)  24.1 us
  transfers between devices with their start and end apart: 8, of which 8 were waited for; matrix products, arithmetic and copies ran while one was open for 32% of the time, Pallas kernels for 0%

profile of v1, /device:TPU:0, one launch (start us, length us, event | category | flops | bytes accessed | tf_op | source)
XLA Modules:
  0.0 921.8 jit_solution(4696724931748309982)
XLA Ops:
  8.9 4.1 broadcast_in_dim.6
  13.0 10.5 %reshape.47 = f32[1280,3,384]{2,0,1:T(8,128)} reshape(f32[10,128,3,3,128]{4,3,1,0,2:T(4,128)} %broadcast_in_dim.6) | data formatting | bytes 11796480 | tf_op jit(solution)/shard_map/reshape | solution.py:38
  23.5 55.8 %all-gather.9.cloned.1.call-done = f32[1280,3,384]{0,2,1:T(8,128)} async-done(((f32[1280,3,96]{0,2,1:T(8,128)}), f32[1280,3,384]{0,2,1:T(8,128)}) %all-gather.9.cloned.1.call-update) | async-done | bytes 5898256 | tf_op jit(solution)/shard_map/all_gather | solution.py:60
  79.3 7.7 copy.73
  87.0 9.3 %mul.30 = f32[1280,3,384]{2,0,1:T(8,128)} multiply(f32[1280,3,384]{2,0,1:T(8,128)} %copy.73, f32[1280,3,384]{2,0,1:T(8,128)} %reshape.47) | non-fusion elementwise | flops 1474560 | bytes 17694720 | tf_op jit(solution)/shard_map/mul | solution.py:60
  96.3 7.8 copy.74
  104.1 52.6 %convolution_bitcast_fusion = f32[2560,1152]{0,1:T(8,128)} fusion(f32[1280,1152]{0,1:T(8,128)} %bitcast.168, f32[2560,1280]{1,0:T(8,128)} %param.7), kind=kOutput, calls=%fused_computation | convolution fusion | flops 45298483200 | bytes 30801920 | tf_op jit(solution)/shard_map/dot_general | solution.py:19
  156.7 13.5 %copy.96 = f32[2560,1152]{1,0:T(8,128)} copy(f32[2560,1152]{0,1:T(8,128)} %convolution_bitcast_fusion) | data formatting | bytes 23592960
  170.6 6.0 broadcast_in_dim.7
  176.6 13.7 %reshape.50 = f32[2560,3,384]{0,2,1:T(8,128)} reshape(f32[20,128,3,3,128]{1,0,4,3,2:T(8,128)} %broadcast_in_dim.7) | data formatting | bytes 23592960 | tf_op jit(solution)/shard_map/reshape | solution.py:38
  191.2 9.7 %mul.32 = f32[2560,3,384]{0,2,1:T(8,128)S(1)} multiply(f32[2560,3,384]{0,2,1:T(8,128)} %all-gather.11.cloned.1.call-done, f32[2560,3,384]{0,2,1:T(8,128)} %reshape.50) | non-fusion elementwise | flops 2949120 | bytes 35389440 | tf_op jit(solution)/shard_map/mul | solution.py:61
  200.9 4.3 copy-done
  205.3 50.0 %convolution_bitcast_fusion.1 = f32[1280,1152]{0,1:T(8,128)} fusion(f32[2560,1152]{0,1:T(8,128)S(1)} %bitcast.159, f32[2560,1280]{1,0:T(8,128)} %param.7), kind=kOutput, calls=%fused_computation.1 | convolution fusion | flops 45298483200 | bytes 30801920 | tf_op jit(solution)/shard_map/dot_general | solution.py:23
  255.3 7.7 copy.98
  263.5 9.2 %fusion.75 = (f32[2560,1,384]{0,2,1:T(8,128)}, f32[2560,1,384]{0,2,1:T(8,128)}, f32[2560,1,384]{0,2,1:T(8,128)}) fusion(f32[2560,3,384]{0,2,1:T(8,128)} %copy-done), kind=kLoop, calls=%fused_computation.101 | loop fusion | bytes 23592960 | tf_op jit(solution)/shard_map/slice | solution.py:78
  272.7 40.8 %reduce-scatter.7.cloned.1.call-done = f32[320,1152]{1,0:T(8,128)} async-done(((f32[2560,1152]{1,0:T(8,128)}), f32[320,1152]{1,0:T(8,128)}) %reduce-scatter.7.cloned.1.call-update) | async-done | bytes 1474576
  313.5 2.1 copy.97
  316.8 3.4 fusion.22
  321.5 3.3 fusion.20
  324.9 4.3 fusion.76
  329.2 52.4 %reduce-scatter.9.cloned.1.call-done = f32[320,1152]{1,0:T(8,128)} async-done(((f32[1280,1152]{1,0:T(8,128)}), f32[320,1152]{1,0:T(8,128)}) %reduce-scatter.9.cloned.1.call-update) | async-done | bytes 1474576
  381.6 2.1 copy.99
  386.3 2.1 copy.104
  388.3 3.2 fusion.18
  391.6 3.4 fusion.12
  395.0 3.2 fusion.51
  399.3 3.2 fusion.49
  402.7 2.1 copy.102
  404.8 2.3 convolution_subtract_fusion.2
  407.9 3.3 fusion.14
  411.2 2.7 fusion.77
  413.8 2.1 copy.106
  416.0 2.1 copy.107
  418.1 2.1 copy.108
  423.1 2.3 pad_maximum_fusion
  427.8 80.8 %all-gather.13.cloned.1.call-done = f32[12288,384]{1,0:T(8,128)} async-done(((f32[384,384]{1,0:T(8,128)}), f32[12288,384]{1,0:T(8,128)}) %all-gather.13.cloned.1.call-update) | async-done | bytes 18874384 | tf_op jit(solution)/shard_map/all_gather | solution.py:13
  508.5 7.3 reduce_sum.29
  516.9 116.8 %all-gather.15.cloned.1.call-done = f32[12288,384]{1,0:T(8,128)} async-done(((f32[384,384]{1,0:T(8,128)}), f32[12288,384]{1,0:T(8,128)}) %all-gather.15.cloned.1.call-update) | async-done | bytes 18874384 | tf_op jit(solution)/shard_map/all_gather | solution.py:13
  633.7 7.3 reduce_sum.31
  642.0 1.4 bitcast_subtract_fusion.2
  643.4 131.2 %all-reduce.3.cloned.1.call-done = (f32[384,384]{1,0:T(8,128)}, f32[384,384]{1,0:T(8,128)}, f32[384,384]{1,0:T(8,128)}, f32[384,384]{1,0:T(8,128)}) async-done(((f32[384,384]{1,0:T(8,128)}, f32[384,384]{1,0:T(8,128)}, f32[384,384]{1,0:T(8,128)}, f32[384,384]{1,0:T(8,128)}), (f32[384,384]{1,0:T(8,128)}, f32[384,384]{1,0:T(8,128)}, f32[384,384]{1,0:T(8,128)}, ...) | async-done | bytes 2359312 | tf_op jit(solution)/shard_map/psum | solution.py:99
  774.6 2.5 fusion.7
  778.5 2.1 fusion.10
  780.7 1.5 fusion.4
  784.6 115.8 %all-gather.17.cloned.1.call-done = f32[12288,384]{1,0:T(8,128)} async-done(((f32[384,384]{1,0:T(8,128)}), f32[12288,384]{1,0:T(8,128)}) %all-gather.17.cloned.1.call-update) | async-done | bytes 18874384 | tf_op jit(solution)/shard_map/all_gather | solution.py:13
  900.5 8.1 reduce_sum.32
  908.6 2.1 copy.87
  910.7 3.3 fusion.9
  (69 shorter events, 22.5 us)
Async XLA Ops:
  7.2 1.5 copy-start.14
  7.2 72.2 %all-gather.9.cloned.1.call-start = ((), (), s32[]{:S(2)}) async-start(), calls=%async_computation.2 | async-start | bytes 7372800 | tf_op jit(solution)/shard_map/all_gather | solution.py:60
  7.9 183.3 %all-gather.11.cloned.1.call-start = ((), (), s32[]{:S(2)}) async-start(), calls=%async_computation.3 | async-start | bytes 13271040 | tf_op jit(solution)/shard_map/all_gather | solution.py:61
  8.7 304.8 %reduce-scatter.7.cloned.1.call-start = ((), (), s32[]{:S(2)}) async-start(), calls=%async_computation.7 | async-start | bytes 13271040
  170.2 211.4 %reduce-scatter.9.cloned.1.call-start = ((), (), s32[]{:S(2)}) async-start(), calls=%async_computation.8 | async-start | bytes 7372800
  200.9 4.3 copy-start
  263.0 245.5 %all-gather.13.cloned.1.call-start = ((), (), s32[]{:S(2)}) async-start(), calls=%async_computation.4 | async-start | bytes 19464192 | tf_op jit(solution)/shard_map/all_gather | solution.py:13
  316.6 3.9 copy-start.2
  320.2 313.5 %all-gather.15.cloned.1.call-start = ((), (), s32[]{:S(2)}) async-start(), calls=%async_computation.5 | async-start | bytes 19464192 | tf_op jit(solution)/shard_map/all_gather | solution.py:13
  324.9 449.7 %all-reduce.3.cloned.1.call-start = ((), (), s32[]{:S(2)}) async-start(), calls=%async_computation.9 | async-start | bytes 4718592 | tf_op jit(solution)/shard_map/psum | solution.py:99
  391.6 6.6 copy-start.1
  391.6 6.6 copy-start.10
  402.5 498.0 %all-gather.17.cloned.1.call-start = ((), (), s32[]{:S(2)}) async-start(), calls=%async_computation.6 | async-start | bytes 19464192 | tf_op jit(solution)/shard_map/all_gather | solution.py:13
  407.1 0.8 copy-start.5
  421.0 2.1 copy-start.6
  423.1 3.4 copy-start.9
  642.0 135.1 %copy-start.3 = (f32[2,384,384]{2,1,0:T(8,128)S(1)}, f32[2,384,384]{2,1,0:T(8,128)}, u32[]{:S(2)}) copy-start(f32[2,384,384]{2,1,0:T(8,128)} %param.10) | copy-start | bytes 3538948
  774.6 2.5 copy-start.13
  774.6 3.9 copy-start.7
  774.6 3.9 copy-start.8
  778.5 2.1 copy-start.12
  778.5 3.7 copy-start.4
  778.5 3.7 copy-start.11
Sparse Core Ops, SparseCore 0:
  9.8 69.4 all-gather.8
  81.0 110.1 all-gather.10
  193.5 119.9 reduce-scatter.6
  316.4 65.2 reduce-scatter.8
  384.5 123.9 all-gather.12
  511.4 122.2 all-gather.14
  639.7 134.8 all-reduce.2
  777.6 122.7 all-gather.16
